TPU v7x, 128 devices: a whole 4x4x4 slice. The times are simulated.
128 devices in a mesh: row: 8 (over x, core), col: 16 (over y, z).
Axes of the slice: x: 4, y: 4, z: 4, core: 2. Of those that a mesh axis runs over, the one named last changes fastest.
Arguments:
- pair: float32 [1024, 1024, 128], P('row', 'col'), may hold values from -6 to 6
- logit_cotangent: bfloat16 [1024, 1024, 64], P('row', 'col'), may hold values from -6 to 6
- tiles: bfloat16 [2048, 1024, 64], P(('row', 'col')), may hold values from -6 to 6
- tile_target: int32 [2048, 1], P(('row', 'col')), may hold values from 0 to 15; in each aligned block of 16 rows (0 to 15, 16 to 31, ...) at most 2 rows name the same one
- tile_square: int32 [2048], P(('row', 'col')), may hold values from 0 to 7
- tile_count: int32 [2048], P(('row', 'col')), may hold values from 1 to 4
- w_template: bfloat16 [64, 128], replicated, may hold values from -0.75 to 0.75
- transition_norm_gain: float32 [128], replicated, may hold values from 0.1 to 1.9
- transition_norm_bias: float32 [128], replicated, may hold values from -3 to 3
- w_gate: bfloat16 [128, 512], replicated, may hold values from -0.5 to 0.5
- w_up: bfloat16 [128, 512], replicated, may hold values from -0.5 to 0.5
- w_out: bfloat16 [512, 128], replicated, may hold values from -0.25 to 0.25
- w_dist: bfloat16 [128, 64], replicated, may hold values from -0.5 to 0.5
Outputs:
- logits: bfloat16 [1024, 1024, 64], P('row', 'col')
- grad_pair: float32 [1024, 1024, 128], P('row', 'col')
- grad_tiles: bfloat16 [2048, 1024, 64], P(('row', 'col'))
- grad_template: float32 [64, 128], replicated
- grad_gain: float32 [128], replicated
- grad_bias: float32 [128], replicated
- grad_gate: float32 [128, 512], replicated
- grad_up: float32 [128, 512], replicated
- grad_out: float32 [512, 128], replicated
- grad_dist: float32 [128, 64], replicated
Inputs may be any that keep to these rules, and one draw needn't show every extreme that they name: `tile_target`: among the 16 tiles of one device no column device is named more than 2 times; some device names one exactly 2 times.
All inputs are finite; a program needn't handle non-finite values.
Results may differ from a plain program's by a relative error of at most 0.0079.
Values may be sent and summed in bfloat16 or wider, within the bound.
A program may use at most 128 MiB of HBM per device.

v0:
```python
import math
import jax
import jax.numpy as jnp
from jax import lax
from jax.sharding import PartitionSpec as P

SQ = 32
CAP = 2


def to_squares(values, across, downward):
    return (
        values.reshape(across, SQ, downward, SQ, -1)
        .transpose(0, 2, 1, 3, 4)
        .reshape(across * downward, SQ * SQ, -1)
    )


def from_squares(values, across, downward):
    return (
        values.reshape(across, downward, SQ, SQ, -1)
        .transpose(0, 2, 1, 3, 4)
        .reshape(across * SQ, downward * SQ, -1)
    )


def norm_intermediates(pair_entries, transition_norm_gain, transition_norm_bias):
    centered_entries = pair_entries - jnp.mean(pair_entries, axis=-1, keepdims=True)
    inverse_deviation = lax.rsqrt(
        jnp.mean(centered_entries * centered_entries, axis=-1, keepdims=True) + 1e-05
    )
    standardized_entries = centered_entries * inverse_deviation
    return (
        standardized_entries,
        inverse_deviation,
        (standardized_entries * transition_norm_gain + transition_norm_bias).astype(jnp.bfloat16),
    )


def transition_forward(
    pair_entries, transition_norm_gain, transition_norm_bias, w_gate, w_up, w_out
):
    standardized_entries, inverse_deviation, normalized_entries = norm_intermediates(
        pair_entries, transition_norm_gain, transition_norm_bias
    )
    gate = jnp.dot(normalized_entries, w_gate, preferred_element_type=jnp.float32)
    upper = jnp.dot(normalized_entries, w_up, preferred_element_type=jnp.float32)
    hidden = (jax.nn.silu(gate) * upper).astype(jnp.bfloat16)
    return pair_entries + jnp.dot(hidden, w_out, preferred_element_type=jnp.float32)


def transition_backward(
    pair_entries, upstream, transition_norm_gain, transition_norm_bias, w_gate, w_up, w_out
):
    standardized_entries, inverse_deviation, normalized_entries = norm_intermediates(
        pair_entries, transition_norm_gain, transition_norm_bias
    )
    gate = jnp.dot(normalized_entries, w_gate, preferred_element_type=jnp.float32)
    upper = jnp.dot(normalized_entries, w_up, preferred_element_type=jnp.float32)
    sigma = jax.nn.sigmoid(gate)
    swish = gate * sigma
    hidden = (swish * upper).astype(jnp.bfloat16)
    up_low = upstream.astype(jnp.bfloat16)
    g_out = jnp.dot(hidden.T, up_low, preferred_element_type=jnp.float32)
    d_hidden = jnp.dot(up_low, w_out.T, preferred_element_type=jnp.float32)
    d_gate = (d_hidden * upper * sigma * (1.0 + gate * (1.0 - sigma))).astype(jnp.bfloat16)
    d_upper = (d_hidden * swish).astype(jnp.bfloat16)
    g_gate = jnp.dot(normalized_entries.T, d_gate, preferred_element_type=jnp.float32)
    g_up = jnp.dot(normalized_entries.T, d_upper, preferred_element_type=jnp.float32)
    normalized_gradient = jnp.dot(d_gate, w_gate.T, preferred_element_type=jnp.float32) + jnp.dot(
        d_upper, w_up.T, preferred_element_type=jnp.float32
    )
    gain_gradient = jnp.sum(normalized_gradient * standardized_entries, axis=0)
    g_bias = jnp.sum(normalized_gradient, axis=0)
    standardized_gradient = normalized_gradient * transition_norm_gain
    entries_gradient = (
        standardized_gradient
        - jnp.mean(standardized_gradient, axis=-1, keepdims=True)
        - standardized_entries
        * jnp.mean(standardized_gradient * standardized_entries, axis=-1, keepdims=True)
    ) * inverse_deviation
    return (upstream + entries_gradient, (gain_gradient, g_bias, g_gate, g_up, g_out))


def mirror(block, row_devs, col_devs):
    rows_here, cols_here, bins = block.shape
    piece = rows_here // col_devs
    devices = row_devs * col_devs
    spread = lax.all_to_all(block, "col", split_axis=0, concat_axis=1, tiled=True)
    split = spread.reshape(piece, devices, piece, bins)
    moved = lax.all_to_all(split, ("row", "col"), split_axis=1, concat_axis=0, tiled=True)
    columns = moved.reshape(devices * piece, piece, bins)
    flipped = columns.transpose(1, 0, 2)
    return lax.all_to_all(flipped, "col", split_axis=1, concat_axis=0, tiled=True)


def per_device(
    pair,
    logit_cotangent,
    tiles,
    tile_target,
    tile_square,
    tile_count,
    w_template,
    transition_norm_gain,
    transition_norm_bias,
    w_gate,
    w_up,
    w_out,
    w_dist,
):
    row_devs = lax.axis_size("row")
    col_devs = lax.axis_size("col")
    rows_here, cols_here, width = pair.shape
    bins = w_dist.shape[1]
    length = rows_here * row_devs
    slots, cells_sq, feature = tiles.shape
    sq_rows = rows_here // SQ
    sq_cols = cols_here // SQ
    squares = sq_rows * sq_cols
    mirrored_cot = mirror(logit_cotangent, row_devs, col_devs)
    target = tile_target[:, 0]
    positions = jnp.arange(slots, dtype=jnp.int32)
    earlier = positions[None, :] < positions[:, None]
    same_target = target[:, None] == target[None, :]
    slot_rank = jnp.sum((same_target & earlier).astype(jnp.int32), axis=1)
    chooser_bool = (
        target[:, None, None] == jnp.arange(col_devs, dtype=jnp.int32)[None, :, None]
    ) & (slot_rank[:, None, None] == jnp.arange(CAP, dtype=jnp.int32)[None, None, :])
    chooser_int = chooser_bool.astype(jnp.int32)
    chooser = chooser_bool.astype(jnp.bfloat16)
    occupied = jnp.sum(chooser_int, axis=0)
    send_ids = jnp.sum(chooser_int * (tile_square + 1)[:, None, None], axis=0) - 1
    send_counts = jnp.sum(chooser_int * tile_count[:, None, None], axis=0) + 1 - occupied
    counts_f = tile_count.astype(jnp.float32)
    proj = jnp.dot(
        tiles.reshape(slots * cells_sq, feature), w_template, preferred_element_type=jnp.float32
    )
    proj = (proj.reshape(slots, cells_sq, width) / counts_f[:, None, None]).astype(jnp.bfloat16)
    payload = jnp.einsum("sdk,spc->dkpc", chooser, proj, preferred_element_type=jnp.float32).astype(
        jnp.bfloat16
    )
    received, got_ids, got_counts = (
        lax.all_to_all(payload, "col", split_axis=0, concat_axis=0, tiled=True),
        lax.all_to_all(send_ids, "col", split_axis=0, concat_axis=0, tiled=True),
        lax.all_to_all(send_counts, "col", split_axis=0, concat_axis=0, tiled=True),
    )
    incoming = col_devs * CAP
    got_ids = got_ids.reshape(incoming)
    proj_in = received.reshape(incoming, cells_sq, width)
    placing = (got_ids[:, None] == jnp.arange(squares, dtype=jnp.int32)[None, :]).astype(
        jnp.bfloat16
    )
    added = jnp.einsum("ns,npc->spc", placing, proj_in, preferred_element_type=jnp.float32)
    z_one = pair + from_squares(added, sq_rows, sq_cols)
    pair_entries = rows_here * cols_here
    block = math.gcd(pair_entries, 2048)
    blocks = pair_entries // block
    z_blocks = z_one.reshape(blocks, block, width)
    z_two = lax.map(
        lambda piece: transition_forward(
            piece, transition_norm_gain, transition_norm_bias, w_gate, w_up, w_out
        ),
        z_blocks,
    )
    z_low = z_two.reshape(pair_entries, width).astype(jnp.bfloat16)
    heads = (
        jnp.dot(z_low, w_dist, preferred_element_type=jnp.float32)
        .astype(jnp.bfloat16)
        .reshape(rows_here, cols_here, bins)
    )
    heads_mirror = mirror(heads, row_devs, col_devs)
    logits = (heads.astype(jnp.float32) + heads_mirror.astype(jnp.float32)).astype(jnp.bfloat16)
    d_heads = (
        (logit_cotangent.astype(jnp.float32) + mirrored_cot.astype(jnp.float32))
        .astype(jnp.bfloat16)
        .reshape(pair_entries, bins)
    )
    dz_two = jnp.dot(d_heads, w_dist.T, preferred_element_type=jnp.float32)
    g_dist = jnp.dot(z_low.T, d_heads, preferred_element_type=jnp.float32)

    def back_block(carry, items):
        piece, upstream = items
        d_piece, grads = transition_backward(
            piece, upstream, transition_norm_gain, transition_norm_bias, w_gate, w_up, w_out
        )
        return (tuple((total + term for total, term in zip(carry, grads))), d_piece)

    hidden_units = w_gate.shape[1]
    start = (
        jnp.zeros((width,), jnp.float32),
        jnp.zeros((width,), jnp.float32),
        jnp.zeros((width, hidden_units), jnp.float32),
        jnp.zeros((width, hidden_units), jnp.float32),
        jnp.zeros((hidden_units, width), jnp.float32),
    )
    sums, dz_one = lax.scan(back_block, start, (z_blocks, dz_two.reshape(blocks, block, width)))
    grad_pair = dz_one.reshape(rows_here, cols_here, width)
    d_squares = to_squares(grad_pair, sq_rows, sq_cols)
    valid = (got_ids >= 0).astype(jnp.float32)
    picked = jnp.take(d_squares, jnp.maximum(got_ids, 0), axis=0)
    d_proj_in = (picked * valid[:, None, None]).astype(jnp.bfloat16)
    returned = lax.all_to_all(
        d_proj_in.reshape(col_devs, CAP, cells_sq, width),
        "col",
        split_axis=0,
        concat_axis=0,
        tiled=True,
    )
    d_proj = jnp.einsum(
        "sdk,dkpc->spc", chooser, returned, preferred_element_type=jnp.float32
    ).astype(jnp.bfloat16)
    g_tile = jnp.dot(
        d_proj.reshape(slots * cells_sq, width), w_template.T, preferred_element_type=jnp.float32
    )
    grad_tiles = (g_tile.reshape(slots, cells_sq, feature) / counts_f[:, None, None]).astype(
        jnp.bfloat16
    )
    per_slot = jnp.einsum("spt,spc->stc", tiles, d_proj, preferred_element_type=jnp.float32)
    g_template = jnp.sum(per_slot / counts_f[:, None, None], axis=0)
    totals = lax.psum(
        (g_template, sums[0], sums[1], sums[2], sums[3], sums[4], g_dist), ("row", "col")
    )
    scale = jnp.float32(length)
    return (
        logits,
        grad_pair,
        grad_tiles,
        totals[0] / scale,
        totals[1] / scale,
        totals[2] / scale,
        totals[3] / scale,
        totals[4] / scale,
        totals[5] / scale,
        totals[6] / scale,
    )


def solution(mesh):
    return jax.shard_map(
        per_device,
        mesh=mesh,
        in_specs=(
            P("row", "col", None),
            P("row", "col", None),
            P(("row", "col"), None, None),
            P(("row", "col"), None),
            P(("row", "col")),
            P(("row", "col")),
            P(),
            P(),
            P(),
            P(),
            P(),
            P(),
            P(),
        ),
        out_specs=(
            P("row", "col", None),
            P("row", "col", None),
            P(("row", "col"), None, None),
            P(),
            P(),
            P(),
            P(),
            P(),
            P(),
            P(),
        ),
        check_vma=False,
    )
```

profile of v0, /device:TPU:1, one launch (start us, length us, event | category | flops | bytes accessed | tf_op | source)
XLA Modules:
  0.0 949.8 jit_solution(895207414862114113)
XLA Ops:
  13.4 8.6 all-to-all-start.5
  23.2 6.2 copy.143
  29.3 8.4 all-to-all-done.5
  48.0 9.8 %all-to-all-start.6 = ((bf16[128,2,2048]{2,1,0:T(2,128)(2,1)}), bf16[128,2,2048]{2,1,0:T(2,128)(2,1)S(1)}, u32[]{:S(2)}, u32[]{:S(2)}) async-start(bf16[128,2,2048]{2,1,0:T(2,128)(2,1)} %reshape.291), calls=%async_computation.6 | async-start | bytes 2097152 | tf_op jit(solution)/shard_map/all_to_all | solution.py:91
  57.8 8.1 convolution_convert_fusion.1
  65.9 8.8 copy.145
  95.0 136.2 %all-to-all-done.1 = bf16[16,2,1024,128]{3,2,1,0:T(8,128)(2,1)} async-done(((bf16[16,2,1024,128]{3,2,1,0:T(8,128)(2,1)}), bf16[16,2,1024,128]{3,2,1,0:T(8,128)(2,1)}, u32[]{:S(2)}, u32[]{:S(2)}) %all-to-all-start.1) | async-done | bytes 8388640 | tf_op jit(solution)/shard_map/all_to_all | solution.py:144
  231.2 9.6 %all-to-all-start.7 = ((bf16[16,2,16384]{2,1,0:T(2,128)(2,1)}), bf16[16,2,16384]{2,1,0:T(2,128)(2,1)}, u32[]{:S(2)}, u32[]{:S(2)}) async-start(bf16[16,2,16384]{2,1,0:T(2,128)(2,1)} %reshape.293), calls=%async_computation.7 | async-start | bytes 2097152 | tf_op jit(solution)/shard_map/all_to_all | solution.py:94
  240.8 12.0 %copy.146 = bf16[1024,128,32]{1,2,0:T(8,128)(2,1)} copy(bf16[1024,128,32]{1,0,2:T(8,128)(2,1)} %bitcast.10) | data formatting | bytes 16777216 | tf_op jit(solution)/shard_map/ns,npc->spc/dot_general | solution.py:154
  262.6 48.9 %while.33 = (s32[]{:T(128)}, bf16[4,2048,128]{2,1,0:T(8,128)(2,1)S(1)}, f32[4,2048,128]{2,1,0:T(8,128)}, f32[128]{0:T(128)S(1)}, f32[128]{0:T(128)S(1)}, /*index...) while((s32[]{:T(128)}, ...), condition=%wide.region_5.6_spmd.clone, body=%wide.region_2.5_spmd.sunk.clone | while | flops 815532032 | bytes 15166569 | solution.py:160
  326.6 6.7 all-to-all-start.2
  344.4 5.7 copy.158
  376.3 12.3 %all-to-all-start.3 = ((bf16[128,2,2048]{2,1,0:T(2,128)(2,1)}), bf16[128,2,2048]{2,1,0:T(2,128)(2,1)}, u32[]{:S(2)}, u32[]{:S(2)}) async-start(bf16[128,2,2048]{2,1,0:T(2,128)(2,1)} %reshape.285), calls=%async_computation.3 | async-start | bytes 2097152 | tf_op jit(solution)/shard_map/all_to_all | solution.py:91
  388.6 68.5 %while.34 = (s32[]{:T(128)}, f32[128]{0:T(128)S(1)}, f32[128]{0:T(128)S(1)}, f32[128,512]{1,0:T(8,128)S(1)}, f32[128,512]{1,0:T(8,128)S(1)}, /*index=5*/f32[512,...) while((s32[]{:T(128)}, f32[128]{0:T(128)S(1)}, ...), condition=%wide.region_13.14_spmd.clone.clone, body=%wide.region_6.13_spmd.clone.sunk.clone | while | flops 2174880000 | bytes 88914152 | solution.py:197
  462.2 10.2 %gather_fusion = f32[32,1024,128]{2,1,0:T(8,128)} fusion(f32[8,1024,128]{2,1,0:T(8,128)} %bitcast.257, s32[1024]{0:T(1024)S(1)} %pad_clamp_fusion), kind=kCustom, calls=%fused_computation | custom fusion | bytes 33554560 | tf_op jit(solution)/shard_map/jit(_take)/gather | solution.py:201
  478.5 7.6 all-to-all-start.4
  486.1 6.9 multiply_convert_fusion.7
  493.0 7.7 copy.168
  502.7 6.0 all-to-all-start.8
  513.9 242.9 %all-reduce.7.cloned.1.call-done = (f32[128,512]{1,0:T(8,128)}, f32[128,512]{1,0:T(8,128)}, f32[512,128]{1,0:T(8,128)}) async-done(((f32[128,512]{1,0:T(8,128)}, f32[128,512]{1,0:T(8,128)}, f32[512,128]{1,0:T(8,128)}), (f32[128,512]{1,0:T(8,128)}, f32[128,512]{1,0:T(8,128)}, f32[512,128]{1,0:T(8,128)})) %all-reduce.7.cloned.1.call-update) | async-done | bytes 786448 | tf_op jit(solution)/shard_map/psum | solution.py:221
  773.8 5.8 copy.153
  787.4 8.6 bitcast_convert_fusion.3
  799.2 6.1 divide_convert_fusion.1
  805.3 133.5 %all-reduce.5.cloned.1.call-done = (f32[64,128]{1,0:T(8,128)}, f32[128]{0:T(128)}, f32[128]{0:T(128)}, f32[128,64]{0,1:T(8,128)}) async-done(((f32[64,128]{1,0:T(8,128)}, f32[128]{0:T(128)}, f32[128]{0:T(128)}, f32[128,64]{0,1:T(8,128)}), (f32[64,128]{1,0:T(8,128)}, f32[128]{0:T(128)}, f32[128]{0:T(128)}, f32[128,64]{0,1:T(8,128)})) %all-reduce.5.cloned.1.call-update) | async-done | bytes 66576 | tf_op jit(solution)/shard_map/psum | solution.py:221
  (252 shorter events, 266.5 us)
Async XLA Ops:
  7.2 50.6 %copy-start = (bf16[64,128]{1,0:T(8,128)(2,1)S(1)}, bf16[64,128]{1,0:T(8,128)(2,1)}, u32[]{:S(2)}) copy-start(bf16[64,128]{1,0:T(8,128)(2,1)} %param.23) | copy-start | bytes 49156
  7.2 14.8 %copy-start.30 = (s32[16]{0:T(128)S(1)}, s32[16]{0:T(128)}, u32[]{:S(2)}) copy-start(s32[16]{0:T(128)} %param.22) | copy-start | bytes 196
  7.2 14.9 %copy-start.28 = (s32[16,1]{0,1:T(1,128)S(1)}, s32[16,1]{0,1:T(1,128)}, u32[]{:S(2)}) copy-start(s32[16,1]{0,1:T(1,128)} %param.20) | copy-start | bytes 196
  7.2 15.1 %copy-start.31 = (s32[16]{0:T(128)S(1)}, s32[16]{0:T(128)}, u32[]{:S(2)}) copy-start(s32[16]{0:T(128)} %param.21) | copy-start | bytes 196
  13.4 24.3 %all-to-all-start.5 = ((bf16[16,2,16384]{2,1,0:T(2,128)(2,1)}), bf16[16,2,16384]{2,1,0:T(2,128)(2,1)S(1)}, u32[]{:S(2)}, u32[]{:S(2)}) async-start(bf16[16,2,16384]{2,1,0:T(2,128)(2,1)} %reshape.289), calls=%async_computation.5 | async-start | bytes 2097152 | tf_op jit(solution)/shard_map/all_to_all | solution.py:89
  22.1 35.7 %copy-start.32 = (f32[16]{0:T(128)}, f32[16]{0:T(128)S(1)}, u32[]{:S(2)}) copy-start(f32[16]{0:T(128)S(1)} %convert_element_type.103) | copy-start | bytes 196
  22.3 35.5 %copy-start.26 = (pred[16,2]{0,1:T(4,128)(4,1)}, pred[16,2]{0,1:T(4,128)(4,1)S(1)}, u32[]{:S(2)}) copy-start(pred[16,2]{0,1:T(4,128)(4,1)S(1)} %iota_compare_fusion.2) | copy-start | bytes 100
  22.4 35.4 %copy-start.23 = (pred[16,16]{1,0:T(8,128)(4,1)}, pred[16,16]{1,0:T(8,128)(4,1)S(1)}, u32[]{:S(2)}) copy-start(pred[16,16]{1,0:T(8,128)(4,1)S(1)} %iota_compare_fusion.1) | copy-start | bytes 772
  37.7 10.3 %all-to-all-start = ((s32[16,1,2]{2,1,0:T(1,128)}), s32[16,1,2]{2,1,0:T(1,128)S(1)}, u32[]{:S(2)}, u32[]{:S(2)}) async-start(s32[16,1,2]{2,1,0:T(1,128)} %copy.142), calls=%async_computation | async-start | bytes 16384 | tf_op jit(solution)/shard_map/all_to_all | solution.py:145
  48.0 28.8 %all-to-all-start.6 = ((bf16[128,2,2048]{2,1,0:T(2,128)(2,1)}), bf16[128,2,2048]{2,1,0:T(2,128)(2,1)S(1)}, u32[]{:S(2)}, u32[]{:S(2)}) async-start(bf16[128,2,2048]{2,1,0:T(2,128)(2,1)} %reshape.291), calls=%async_computation.6 | async-start | bytes 2097152 | tf_op jit(solution)/shard_map/all_to_all | solution.py:91
  77.7 153.5 %all-to-all-start.1 = ((bf16[16,2,1024,128]{3,2,1,0:T(8,128)(2,1)}), bf16[16,2,1024,128]{3,2,1,0:T(8,128)(2,1)}, u32[]{:S(2)}, u32[]{:S(2)}) async-start(bf16[16,2,1024,128]{3,2,1,0:T(8,128)(2,1)} %copy.145), calls=%async_computation.1 | async-start | bytes 16777216 | tf_op jit(solution)/shard_map/all_to_all | solution.py:144
  231.2 95.4 %all-to-all-start.7 = ((bf16[16,2,16384]{2,1,0:T(2,128)(2,1)}), bf16[16,2,16384]{2,1,0:T(2,128)(2,1)}, u32[]{:S(2)}, u32[]{:S(2)}) async-start(bf16[16,2,16384]{2,1,0:T(2,128)(2,1)} %reshape.293), calls=%async_computation.7 | async-start | bytes 2097152 | tf_op jit(solution)/shard_map/all_to_all | solution.py:94
  262.6 49.0 %copy-start.18 = (bf16[128,64]{0,1:T(8,128)(2,1)S(1)}, bf16[128,64]{0,1:T(8,128)(2,1)}, u32[]{:S(2)}) copy-start(bf16[128,64]{0,1:T(8,128)(2,1)} %param.29) | copy-start | bytes 49156
  326.6 38.7 %all-to-all-start.2 = ((bf16[16,2,16384]{2,1,0:T(2,128)(2,1)}), bf16[16,2,16384]{2,1,0:T(2,128)(2,1)}, u32[]{:S(2)}, u32[]{:S(2)}) async-start(bf16[16,2,16384]{2,1,0:T(2,128)(2,1)} %reshape.283), calls=%async_computation.2 | async-start | bytes 2097152 | tf_op jit(solution)/shard_map/all_to_all | solution.py:89
  376.3 96.1 %all-to-all-start.3 = ((bf16[128,2,2048]{2,1,0:T(2,128)(2,1)}), bf16[128,2,2048]{2,1,0:T(2,128)(2,1)}, u32[]{:S(2)}, u32[]{:S(2)}) async-start(bf16[128,2,2048]{2,1,0:T(2,128)(2,1)} %reshape.285), calls=%async_computation.3 | async-start | bytes 2097152 | tf_op jit(solution)/shard_map/all_to_all | solution.py:91
  472.4 13.7 %copy-start.20 = (f32[16,2]{1,0:T(8,128)S(1)}, f32[16,2]{1,0:T(8,128)}, u32[]{:S(2)}) copy-start(f32[16,2]{1,0:T(8,128)} %copy.167) | copy-start | bytes 388
  472.4 13.7 %copy-start.25 = (pred[16,2]{1,0:T(8,128)(4,1)S(1)}, pred[16,2]{1,0:T(8,128)(4,1)}, u32[]{:S(2)}) copy-start(pred[16,2]{1,0:T(8,128)(4,1)} %copy.163) | copy-start | bytes 100
  478.5 23.2 %all-to-all-start.4 = ((bf16[16,2,16384]{2,1,0:T(2,128)(2,1)}), bf16[16,2,16384]{2,1,0:T(2,128)(2,1)S(1)}, u32[]{:S(2)}, u32[]{:S(2)}) async-start(bf16[16,2,16384]{2,1,0:T(2,128)(2,1)} %reshape.287), calls=%async_computation.4 | async-start | bytes 2097152 | tf_op jit(solution)/shard_map/all_to_all | solution.py:94
  500.8 12.0 %copy-start.3 = (bf16[4,2048,128]{2,1,0:T(8,128)(2,1)S(1)}, bf16[4,2048,128]{2,1,0:T(8,128)(2,1)}, u32[]{:S(2)}) copy-start(bf16[4,2048,128]{2,1,0:T(8,128)(2,1)} %copy-done.2) | copy-start | bytes 6291460
  502.7 284.7 %all-to-all-start.8 = ((bf16[16,2,1024,128]{3,1,2,0:T(2,128)(2,1)}), bf16[16,2,1024,128]{3,1,2,0:T(2,128)(2,1)}, u32[]{:S(2)}, u32[]{:S(2)}) async-start(bf16[16,2,1024,128]{3,1,2,0:T(2,128)(2,1)} %copy.168), calls=%async_computation.8 | async-start | bytes 16777216 | tf_op jit(solution)/shard_map/all_to_all | solution.py:203
  508.7 248.1 %all-reduce.7.cloned.1.call-start = ((), (), s32[]{:S(2)}) async-start(), calls=%async_computation.10 | async-start | bytes 1572864 | tf_op jit(solution)/shard_map/psum | solution.py:221
  509.4 429.4 %all-reduce.5.cloned.1.call-start = ((), (), s32[]{:S(2)}) async-start(), calls=%async_computation.9 | async-start | bytes 133120 | tf_op jit(solution)/shard_map/psum | solution.py:221
  787.4 8.7 copy-start.15
  787.4 8.7 copy-start.33
  (27 other events, 98.5 us)
Sparse Core Ops, SparseCore 0:
  515.7 241.0 all-reduce.6
  799.3 139.4 all-reduce.4
where the time goes:
time: 961 us; the launch traced here: 950 us
  waiting for transfers between devices  527 us (55%)
  local copies, waits for them, and re-layouts  163 us (17%)
  matrix products  104 us (11%)
  other arithmetic  70.3 us (7%)
  starting transfers between devices  70.2 us (7%)
  between operations  14.9 us (2%)
    psum x2, waiting for transfers between devices, per_device(): lax.psum((g_template, sums[0], sums[1], sums[2], sums[3], sums[4], g_dist...  376 us
    all_to_all x1, waiting for transfers between devices, per_device(): lax.all_to_all(payload, 'col', split_axis=0, concat_axis=0, tiled=True)  136 us
    unnamed x79, local copies, waits for them, and re-layouts  56.9 us
    all_to_all x2, starting transfers between devices, mirror(): lax.all_to_all(split, ('row', 'col'), split_axis=1, concat_axis=0, tiled=...  22.1 us
  transfers between devices with their start and end apart: 11, of which 7 were waited for; matrix products, arithmetic and copies ran while one was open for 31% of the time, Pallas kernels for 0%

commit v1 on v0

--- a/solution.py
+++ b/solution.py
@@ -219,7 +219,7 @@
     per_slot = jnp.einsum("spt,spc->stc", tiles, d_proj, preferred_element_type=jnp.float32)
     g_template = jnp.sum(per_slot / counts_f[:, None, None], axis=0)
     totals = lax.psum(
-        (g_template, sums[0], sums[1], sums[2], sums[3], sums[4], g_dist), ("row", "col")
+        lax.psum((g_template, sums[0], sums[1], sums[2], sums[3], sums[4], g_dist), "row"), "col"
     )
     scale = jnp.float32(length)
     return (

time: 961 us -> 903 us (0.940)
  waiting for transfers between devices: 527 us -> 467 us
    psum x2, waiting for transfers between devices: 376 us -> 117 us  [per_device(): lax.psum((g_template, sums[0], sums[1], sums[2], sums[3], sums[4], g_dist...]
    psum x0 -> x2, waiting for transfers between devices: none -> 201 us  [per_device(): lax.psum(lax.psum((g_template, sums[0], sums[1], sums[2], sums[3], sums[4...]
  transfers between devices with their start and end apart: 11 -> 13, of which waited for: 7 -> 9; matrix products, arithmetic and copies ran while one was open for 31% -> 33% of each run, Pallas kernels for 0% -> 0%
where the time goes in v1:
time: 903 us; the launch traced here: 891 us
  waiting for transfers between devices  467 us (52%)
  local copies, waits for them, and re-layouts  162 us (18%)
  matrix products  104 us (12%)
  starting transfers between devices  70.6 us (8%)
  other arithmetic  70.3 us (8%)
  between operations  14.8 us (2%)
    psum x2, waiting for transfers between devices, per_device(): lax.psum(lax.psum((g_template, sums[0], sums[1], sums[2], sums[3], sums[4...  201 us
    all_to_all x1, waiting for transfers between devices, per_device(): lax.all_to_all(payload, 'col', split_axis=0, concat_axis=0, tiled=True)  135 us
    psum x2, waiting for transfers between devices, per_device(): lax.psum((g_template, sums[0], sums[1], sums[2], sums[3], sums[4], g_dist...  117 us
    unnamed x79, local copies, waits for them, and re-layouts  56.7 us
    all_to_all x2, starting transfers between devices, mirror(): lax.all_to_all(split, ('row', 'col'), split_axis=1, concat_axis=0, tiled=...  22.2 us
    dot_general x4, matrix products, transition_forward(): jnp.dot(hidden, w_out, preferred_element_type=jnp.float32)  18.7 us
  transfers between devices with their start and end apart: 13, of which 9 were waited for; matrix products, arithmetic and copies ran while one was open for 33% of the time, Pallas kernels for 0%

profile of v1, /device:TPU:1, one launch (start us, length us, event | category | flops | bytes accessed | tf_op | source)
XLA Modules:
  0.0 890.8 jit_solution(8343681680859101600)
XLA Ops:
  13.4 8.6 all-to-all-start.5
  23.2 6.2 copy.143
  29.3 8.4 all-to-all-done.5
  48.0 9.8 %all-to-all-start.6 = ((bf16[128,2,2048]{2,1,0:T(2,128)(2,1)}), bf16[128,2,2048]{2,1,0:T(2,128)(2,1)S(1)}, u32[]{:S(2)}, u32[]{:S(2)}) async-start(bf16[128,2,2048]{2,1,0:T(2,128)(2,1)} %reshape.291), calls=%async_computation.6 | async-start | bytes 2097152 | tf_op jit(solution)/shard_map/all_to_all | solution.py:91
  57.8 8.1 convolution_convert_fusion.1
  65.9 8.8 copy.145
  94.7 135.2 %all-to-all-done.1 = bf16[16,2,1024,128]{3,2,1,0:T(8,128)(2,1)} async-done(((bf16[16,2,1024,128]{3,2,1,0:T(8,128)(2,1)}), bf16[16,2,1024,128]{3,2,1,0:T(8,128)(2,1)}, u32[]{:S(2)}, u32[]{:S(2)}) %all-to-all-start.1) | async-done | bytes 8388640 | tf_op jit(solution)/shard_map/all_to_all | solution.py:144
  229.9 10.6 %all-to-all-start.7 = ((bf16[16,2,16384]{2,1,0:T(2,128)(2,1)}), bf16[16,2,16384]{2,1,0:T(2,128)(2,1)}, u32[]{:S(2)}, u32[]{:S(2)}) async-start(bf16[16,2,16384]{2,1,0:T(2,128)(2,1)} %reshape.293), calls=%async_computation.7 | async-start | bytes 2097152 | tf_op jit(solution)/shard_map/all_to_all | solution.py:94
  240.5 12.0 %copy.146 = bf16[1024,128,32]{1,2,0:T(8,128)(2,1)} copy(bf16[1024,128,32]{1,0,2:T(8,128)(2,1)} %bitcast.10) | data formatting | bytes 16777216 | tf_op jit(solution)/shard_map/ns,npc->spc/dot_general | solution.py:154
  262.3 49.2 %while.33 = (s32[]{:T(128)}, bf16[4,2048,128]{2,1,0:T(8,128)(2,1)S(1)}, f32[4,2048,128]{2,1,0:T(8,128)}, f32[128]{0:T(128)S(1)}, f32[128]{0:T(128)S(1)}, /*index...) while((s32[]{:T(128)}, ...), condition=%wide.region_5.6_spmd.clone, body=%wide.region_2.5_spmd.sunk.clone | while | flops 815532032 | bytes 15166569 | solution.py:160
  326.5 6.6 all-to-all-start.2
  376.2 12.4 %all-to-all-start.3 = ((bf16[128,2,2048]{2,1,0:T(2,128)(2,1)}), bf16[128,2,2048]{2,1,0:T(2,128)(2,1)}, u32[]{:S(2)}, u32[]{:S(2)}) async-start(bf16[128,2,2048]{2,1,0:T(2,128)(2,1)} %reshape.285), calls=%async_computation.3 | async-start | bytes 2097152 | tf_op jit(solution)/shard_map/all_to_all | solution.py:91
  388.6 68.5 %while.34 = (s32[]{:T(128)}, f32[128]{0:T(128)S(1)}, f32[128]{0:T(128)S(1)}, f32[128,512]{1,0:T(8,128)S(1)}, f32[128,512]{1,0:T(8,128)S(1)}, /*index=5*/f32[512,...) while((s32[]{:T(128)}, f32[128]{0:T(128)S(1)}, ...), condition=%wide.region_13.14_spmd.clone.clone, body=%wide.region_6.13_spmd.clone.sunk.clone | while | flops 2174880000 | bytes 88914152 | solution.py:197
  462.2 10.2 %gather_fusion = f32[32,1024,128]{2,1,0:T(8,128)} fusion(f32[8,1024,128]{2,1,0:T(8,128)} %bitcast.257, s32[1024]{0:T(1024)S(1)} %pad_clamp_fusion), kind=kCustom, calls=%fused_computation | custom fusion | bytes 33554560 | tf_op jit(solution)/shard_map/jit(_take)/gather | solution.py:201
  478.4 7.4 all-to-all-start.4
  485.9 6.9 multiply_convert_fusion.7
  492.8 7.7 copy.168
  502.5 5.9 all-to-all-start.8
  509.1 67.9 %all-reduce.15.cloned.1.call-done = (f32[128,512]{1,0:T(8,128)}, f32[128,512]{1,0:T(8,128)}, f32[512,128]{1,0:T(8,128)}) async-done(((f32[128,512]{1,0:T(8,128)}, f32[128,512]{1,0:T(8,128)}, f32[512,128]{1,0:T(8,128)}), (f32[128,512]{1,0:T(8,128)}, f32[128,512]{1,0:T(8,128)}, f32[512,128]{1,0:T(8,128)})) %all-reduce.15.cloned.1.call-update) | async-done | bytes 786448 | tf_op jit(solution)/shard_map/psum | solution.py:222
  581.5 123.6 %all-reduce.11.cloned.1.call-done = (f32[128,512]{1,0:T(8,128)}, f32[128,512]{1,0:T(8,128)}, f32[512,128]{1,0:T(8,128)}) async-done(((f32[128,512]{1,0:T(8,128)}, f32[128,512]{1,0:T(8,128)}, f32[512,128]{1,0:T(8,128)}), (f32[128,512]{1,0:T(8,128)}, f32[128,512]{1,0:T(8,128)}, f32[512,128]{1,0:T(8,128)})) %all-reduce.11.cloned.1.call-update) | async-done | bytes 786448 | tf_op jit(solution)/shard_map/psum | solution.py:221
  727.9 8.6 bitcast_convert_fusion.3
  747.4 48.7 %all-reduce.13.cloned.1.call-done = (f32[64,128]{1,0:T(8,128)}, f32[128]{0:T(128)}, f32[128]{0:T(128)}, f32[128,64]{0,1:T(8,128)}) async-done(((f32[64,128]{1,0:T(8,128)}, f32[128]{0:T(128)}, f32[128]{0:T(128)}, f32[128,64]{0,1:T(8,128)}), (f32[64,128]{1,0:T(8,128)}, f32[128]{0:T(128)}, f32[128]{0:T(128)}, f32[128,64]{0,1:T(8,128)})) %all-reduce.13.cloned.1.call-update) | async-done | bytes 66576 | tf_op jit(solution)/shard_map/psum | solution.py:222
  796.0 6.1 divide_convert_fusion.1
  802.2 77.8 %all-reduce.9.cloned.1.call-done = (f32[64,128]{1,0:T(8,128)}, f32[128]{0:T(128)}, f32[128]{0:T(128)}, f32[128,64]{0,1:T(8,128)}) async-done(((f32[64,128]{1,0:T(8,128)}, f32[128]{0:T(128)}, f32[128]{0:T(128)}, f32[128,64]{0,1:T(8,128)}), (f32[64,128]{1,0:T(8,128)}, f32[128]{0:T(128)}, f32[128]{0:T(128)}, f32[128,64]{0,1:T(8,128)})) %all-reduce.9.cloned.1.call-update) | async-done | bytes 66576 | tf_op jit(solution)/shard_map/psum | solution.py:221
  (258 shorter events, 277.5 us)
Async XLA Ops:
  7.2 50.6 %copy-start = (bf16[64,128]{1,0:T(8,128)(2,1)S(1)}, bf16[64,128]{1,0:T(8,128)(2,1)}, u32[]{:S(2)}) copy-start(bf16[64,128]{1,0:T(8,128)(2,1)} %param.23) | copy-start | bytes 49156
  7.2 14.8 %copy-start.30 = (s32[16]{0:T(128)S(1)}, s32[16]{0:T(128)}, u32[]{:S(2)}) copy-start(s32[16]{0:T(128)} %param.22) | copy-start | bytes 196
  7.2 14.9 %copy-start.28 = (s32[16,1]{0,1:T(1,128)S(1)}, s32[16,1]{0,1:T(1,128)}, u32[]{:S(2)}) copy-start(s32[16,1]{0,1:T(1,128)} %param.20) | copy-start | bytes 196
  7.2 15.1 %copy-start.31 = (s32[16]{0:T(128)S(1)}, s32[16]{0:T(128)}, u32[]{:S(2)}) copy-start(s32[16]{0:T(128)} %param.21) | copy-start | bytes 196
  13.4 24.3 %all-to-all-start.5 = ((bf16[16,2,16384]{2,1,0:T(2,128)(2,1)}), bf16[16,2,16384]{2,1,0:T(2,128)(2,1)S(1)}, u32[]{:S(2)}, u32[]{:S(2)}) async-start(bf16[16,2,16384]{2,1,0:T(2,128)(2,1)} %reshape.289), calls=%async_computation.5 | async-start | bytes 2097152 | tf_op jit(solution)/shard_map/all_to_all | solution.py:89
  22.1 35.7 %copy-start.32 = (f32[16]{0:T(128)}, f32[16]{0:T(128)S(1)}, u32[]{:S(2)}) copy-start(f32[16]{0:T(128)S(1)} %convert_element_type.103) | copy-start | bytes 196
  22.3 35.5 %copy-start.26 = (pred[16,2]{0,1:T(4,128)(4,1)}, pred[16,2]{0,1:T(4,128)(4,1)S(1)}, u32[]{:S(2)}) copy-start(pred[16,2]{0,1:T(4,128)(4,1)S(1)} %iota_compare_fusion.2) | copy-start | bytes 100
  22.4 35.4 %copy-start.23 = (pred[16,16]{1,0:T(8,128)(4,1)}, pred[16,16]{1,0:T(8,128)(4,1)S(1)}, u32[]{:S(2)}) copy-start(pred[16,16]{1,0:T(8,128)(4,1)S(1)} %iota_compare_fusion.1) | copy-start | bytes 772
  37.7 10.3 %all-to-all-start = ((s32[16,1,2]{2,1,0:T(1,128)}), s32[16,1,2]{2,1,0:T(1,128)S(1)}, u32[]{:S(2)}, u32[]{:S(2)}) async-start(s32[16,1,2]{2,1,0:T(1,128)} %copy.142), calls=%async_computation | async-start | bytes 16384 | tf_op jit(solution)/shard_map/all_to_all | solution.py:145
  48.0 28.8 %all-to-all-start.6 = ((bf16[128,2,2048]{2,1,0:T(2,128)(2,1)}), bf16[128,2,2048]{2,1,0:T(2,128)(2,1)S(1)}, u32[]{:S(2)}, u32[]{:S(2)}) async-start(bf16[128,2,2048]{2,1,0:T(2,128)(2,1)} %reshape.291), calls=%async_computation.6 | async-start | bytes 2097152 | tf_op jit(solution)/shard_map/all_to_all | solution.py:91
  77.7 152.3 %all-to-all-start.1 = ((bf16[16,2,1024,128]{3,2,1,0:T(8,128)(2,1)}), bf16[16,2,1024,128]{3,2,1,0:T(8,128)(2,1)}, u32[]{:S(2)}, u32[]{:S(2)}) async-start(bf16[16,2,1024,128]{3,2,1,0:T(8,128)(2,1)} %copy.145), calls=%async_computation.1 | async-start | bytes 16777216 | tf_op jit(solution)/shard_map/all_to_all | solution.py:144
  229.9 96.6 %all-to-all-start.7 = ((bf16[16,2,16384]{2,1,0:T(2,128)(2,1)}), bf16[16,2,16384]{2,1,0:T(2,128)(2,1)}, u32[]{:S(2)}, u32[]{:S(2)}) async-start(bf16[16,2,16384]{2,1,0:T(2,128)(2,1)} %reshape.293), calls=%async_computation.7 | async-start | bytes 2097152 | tf_op jit(solution)/shard_map/all_to_all | solution.py:94
  262.3 49.2 %copy-start.18 = (bf16[128,64]{0,1:T(8,128)(2,1)S(1)}, bf16[128,64]{0,1:T(8,128)(2,1)}, u32[]{:S(2)}) copy-start(bf16[128,64]{0,1:T(8,128)(2,1)} %param.29) | copy-start | bytes 49156
  326.5 38.7 %all-to-all-start.2 = ((bf16[16,2,16384]{2,1,0:T(2,128)(2,1)}), bf16[16,2,16384]{2,1,0:T(2,128)(2,1)}, u32[]{:S(2)}, u32[]{:S(2)}) async-start(bf16[16,2,16384]{2,1,0:T(2,128)(2,1)} %reshape.283), calls=%async_computation.2 | async-start | bytes 2097152 | tf_op jit(solution)/shard_map/all_to_all | solution.py:89
  376.2 96.2 %all-to-all-start.3 = ((bf16[128,2,2048]{2,1,0:T(2,128)(2,1)}), bf16[128,2,2048]{2,1,0:T(2,128)(2,1)}, u32[]{:S(2)}, u32[]{:S(2)}) async-start(bf16[128,2,2048]{2,1,0:T(2,128)(2,1)} %reshape.285), calls=%async_computation.3 | async-start | bytes 2097152 | tf_op jit(solution)/shard_map/all_to_all | solution.py:91
  472.4 13.5 %copy-start.20 = (f32[16,2]{1,0:T(8,128)S(1)}, f32[16,2]{1,0:T(8,128)}, u32[]{:S(2)}) copy-start(f32[16,2]{1,0:T(8,128)} %copy.167) | copy-start | bytes 388
  472.4 13.5 %copy-start.25 = (pred[16,2]{1,0:T(8,128)(4,1)S(1)}, pred[16,2]{1,0:T(8,128)(4,1)}, u32[]{:S(2)}) copy-start(pred[16,2]{1,0:T(8,128)(4,1)} %copy.163) | copy-start | bytes 100
  478.4 23.1 %all-to-all-start.4 = ((bf16[16,2,16384]{2,1,0:T(2,128)(2,1)}), bf16[16,2,16384]{2,1,0:T(2,128)(2,1)S(1)}, u32[]{:S(2)}, u32[]{:S(2)}) async-start(bf16[16,2,16384]{2,1,0:T(2,128)(2,1)} %reshape.287), calls=%async_computation.4 | async-start | bytes 2097152 | tf_op jit(solution)/shard_map/all_to_all | solution.py:94
  502.5 225.5 %all-to-all-start.8 = ((bf16[16,2,1024,128]{3,1,2,0:T(2,128)(2,1)}), bf16[16,2,1024,128]{3,1,2,0:T(2,128)(2,1)}, u32[]{:S(2)}, u32[]{:S(2)}) async-start(bf16[16,2,1024,128]{3,1,2,0:T(2,128)(2,1)} %copy.168), calls=%async_computation.8 | async-start | bytes 16777216 | tf_op jit(solution)/shard_map/all_to_all | solution.py:203
  508.3 72.1 %copy-start.3 = (bf16[4,2048,128]{2,1,0:T(8,128)(2,1)S(1)}, bf16[4,2048,128]{2,1,0:T(8,128)(2,1)}, u32[]{:S(2)}) copy-start(bf16[4,2048,128]{2,1,0:T(8,128)(2,1)} %copy-done.2) | copy-start | bytes 6291460
  508.3 68.7 %all-reduce.15.cloned.1.call-start = ((), (), s32[]{:S(2)}) async-start(), calls=%async_computation.12 | async-start | bytes 1572864 | tf_op jit(solution)/shard_map/psum | solution.py:222
  509.1 196.1 %all-reduce.11.cloned.1.call-start = ((), (), s32[]{:S(2)}) async-start(), calls=%async_computation.10 | async-start | bytes 1572864 | tf_op jit(solution)/shard_map/psum | solution.py:221
  577.0 219.0 %all-reduce.13.cloned.1.call-start = ((), (), s32[]{:S(2)}) async-start(), calls=%async_computation.11 | async-start | bytes 133120 | tf_op jit(solution)/shard_map/psum | solution.py:222
  739.8 140.2 %all-reduce.9.cloned.1.call-start = ((), (), s32[]{:S(2)}) async-start(), calls=%async_computation.9 | async-start | bytes 133120 | tf_op jit(solution)/shard_map/psum | solution.py:221
  (29 other events, 109.2 us)
Sparse Core Ops, SparseCore 0:
  512.8 64.1 all-reduce.14
  580.6 124.5 all-reduce.10
  739.9 56.0 all-reduce.12
  799.5 80.3 all-reduce.8
